TPU v7x, 128 devices: a whole 4x4x4 slice. The times are simulated.
128 devices in a mesh: dp: 8 (over y, core), queue: 16 (over z, x).
Axes of the slice: x: 4, y: 4, z: 4, core: 2. Of those that a mesh axis runs over, the one named last changes fastest.
Arguments:
- queue_keys: bfloat16 [524288, 768], P(('dp', 'queue')), may hold values from -2.5 to 2.5
- fresh_keys: bfloat16 [1024, 768], P(('dp', 'queue')), may hold values from -4 to 4
- slots: int32 [1024], P(('dp', 'queue')), may hold values from 0 to 524287, as said below
- queries: bfloat16 [1024, 768], P('dp'), may hold values from -40 to 40
- positives: int32 [1024], P('dp'), may hold values from 0 to 1023
Outputs:
- query_grad: float32 [1024, 768], P(('dp', 'queue'))
- mean_loss: float32 [], replicated
- new_queue: bfloat16 [524288, 768], P(('dp', 'queue'))
Inputs may be any that keep to these rules, and one draw needn't show every extreme that they name: The 1024 slots are distinct.
All inputs are finite; a program needn't handle non-finite values.
Results may differ from a plain program's by a relative error of at most 0.0035.
Values may be sent and summed in bfloat16 or wider, within the bound.
A program may use at most 128 MiB of HBM per device.

v0:
```python
import jax
import jax.numpy as jnp
from jax import lax
from jax.sharding import PartitionSpec as P


def score_rows(query_rows, key_rows):
    return lax.dot_general(
        query_rows, key_rows, (((1,), (1,)), ((), ())), preferred_element_type=jnp.float32
    )


def shards(queue_keys, fresh_keys, slots, queries, positives):
    all_queries = lax.all_gather(queries, "dp", axis=0, tiled=True)
    fresh_all, slots_all = (
        lax.all_gather(fresh_keys, ("dp", "queue"), axis=0, tiled=True),
        lax.all_gather(slots, ("dp", "queue"), axis=0, tiled=True),
    )
    queue_scores = score_rows(all_queries, queue_keys)
    fresh_scores = score_rows(all_queries, fresh_keys)
    local_top = jnp.maximum(jnp.max(queue_scores, axis=1), jnp.max(fresh_scores, axis=1))
    row_top = lax.pmax(local_top, ("dp", "queue"))
    queue_exp = jnp.exp(queue_scores - row_top[:, None])
    fresh_exp = jnp.exp(fresh_scores - row_top[:, None])
    local_sum = jnp.sum(queue_exp, axis=1) + jnp.sum(fresh_exp, axis=1)
    sum_exp = lax.psum(local_sum, ("dp", "queue"))
    queue_weights = queue_exp.astype(jnp.bfloat16)
    fresh_weights = fresh_exp.astype(jnp.bfloat16)
    dp_size = lax.axis_size("dp")
    queue_size = lax.axis_size("queue")
    own_rows = all_queries.shape[0] // (dp_size * queue_size)
    pulled = lax.psum_scatter(
        jnp.dot(queue_weights, queue_keys, preferred_element_type=jnp.float32)
        + jnp.dot(fresh_weights, fresh_keys, preferred_element_type=jnp.float32),
        ("dp", "queue"),
        scatter_dimension=0,
        tiled=True,
    )
    queue_index = lax.axis_index("queue")
    device_index = lax.axis_index("dp") * queue_size + queue_index
    row_start = device_index * own_rows
    top_rows = lax.dynamic_slice_in_dim(row_top, row_start, own_rows, 0)
    total_rows = lax.dynamic_slice_in_dim(sum_exp, row_start, own_rows, 0)
    local_start = queue_index * own_rows
    positive_rows = lax.dynamic_slice_in_dim(positives, local_start, own_rows, 0)
    query_rows = lax.dynamic_slice_in_dim(queries, local_start, own_rows, 0)
    positive_keys = jnp.take(fresh_all, positive_rows, axis=0).astype(jnp.float32)
    query_grad = pulled / total_rows[:, None] - positive_keys
    positive_scores = jnp.sum(query_rows.astype(jnp.float32) * positive_keys, axis=1)
    loss_part = jnp.sum(top_rows + jnp.log(total_rows) - positive_scores)
    loss_sum = lax.psum(loss_part, ("dp", "queue"))
    mean_loss = loss_sum / (own_rows * dp_size * queue_size)
    held_rows = queue_keys.shape[0]
    local_slot = slots_all - device_index * held_rows
    inside = (local_slot >= 0) & (local_slot < held_rows)
    target = jnp.where(inside, local_slot, held_rows)
    new_queue = queue_keys.at[target].set(fresh_all, mode="drop")
    return (query_grad, mean_loss, new_queue)


def solution(mesh):
    placed = (
        P(("dp", "queue"), None),
        P(("dp", "queue"), None),
        P(("dp", "queue")),
        P("dp", None),
        P("dp"),
    )
    return jax.shard_map(
        shards,
        mesh=mesh,
        in_specs=placed,
        out_specs=(P(("dp", "queue"), None), P(), P(("dp", "queue"), None)),
        check_vma=False,
    )
```

profile of v0, /device:TPU:1, one launch (start us, length us, event | category | flops | bytes accessed | tf_op | source)
XLA Modules:
  0.0 360.9 jit_solution(16796866037747466775)
XLA Ops:
  7.2 0.0 all-gather.3.cloned.1.call-start
  7.2 5.9 %copy.11 = bf16[4096,768]{1,0:T(8,128)(2,1)} copy(bf16[4096,768]{1,0:T(8,128)(2,1)} %param.5) | data formatting | bytes 12582912
  13.1 0.0 all-gather.3.cloned.1.call-update
  13.1 0.0 all-gather.5.cloned.1.call-start
  13.2 0.7 all-gather.5.cloned.1.call-update
  13.9 0.0 copy-start.1
  13.9 0.0 reduce-scatter.2.cloned.1.call-start
  13.9 27.3 %all-gather.3.cloned.1.call-done = bf16[1024,768]{1,0:T(8,128)(2,1)} async-done(((bf16[128,768]{1,0:T(8,128)(2,1)}), bf16[1024,768]{1,0:T(8,128)(2,1)}) %all-gather.3.cloned.1.call-update) | async-done | bytes 1572880 | tf_op jit(solution)/shard_map/all_gather | solution.py:14
  41.3 0.0 copy-start
  41.3 13.3 %fusion.10 = (f32[1024]{0:T(1024)S(1)}, f32[1024,4096]{1,0:T(8,128)}) fusion(bf16[1024,768]{1,0:T(8,128)(2,1)} %all-gather.3.cloned.1.call-done, bf16[4096,768]{1,0:T(8,128)(2,1)} %copy.11), kind=kOutput, calls=%fused_computation.21 | convolution fusion | flops 6446644224 | bytes 24645632 | tf_op jit(solution)/shard_map/dot_general | solution.py:8
  54.6 0.0 copy-done.1
  54.6 0.0 copy-done
  54.6 0.5 fusion.11
  55.1 64.9 %pmax.7 = f32[1024]{0:T(1024)S(1)} all-reduce(f32[1024]{0:T(1024)S(1)} %max.5), channel_id=1, replica_groups=mesh['dp'=8,'queue'=16] {'dp','queue'}, use_global_device_ids=true, to_apply=%region_2.0 | all-reduce | flops 1024 | bytes 8192 | tf_op jit(solution)/shard_map/pmax | solution.py:22
  120.1 12.3 %fusion.2 = f32[1024,768]{1,0:T(8,128)S(1)} fusion(bf16[4096,768]{1,0:T(8,128)(2,1)} %copy.11, f32[1024,4096]{1,0:T(8,128)} %get-tuple-element.8, f32[1024]{0:T(1024)S(1)} %pmax.7), kind=kOutput, calls=%fused_computation.5 | convolution fusion | flops 6450839552 | bytes 26218496 | tf_op jit(solution)/shard_map/dot_general | solution.py:33
  132.3 0.0 copy-start.3
  132.4 0.0 copy-start.2
  132.4 2.3 convolution_add_fusion
  134.7 0.0 reduce-scatter.2.cloned.1.call-update
  134.7 0.0 copy-done.3
  134.7 0.2 dynamic-update-slice
  135.0 64.1 %all-reduce = s32[1024]{0:T(1024)S(1)} all-reduce(s32[1024]{0:T(1024)S(1)} %dynamic-update-slice), channel_id=1, replica_groups=mesh['dp'=8,'queue'=16] {'dp','queue'}, use_global_device_ids=true, to_apply=%add | all-reduce | flops 1024 | bytes 8192
  199.1 0.0 copy-done.2
  199.1 0.1 compare_and_fusion
  199.2 8.2 %fusion = f32[1024]{0:T(1024)S(1)} fusion(f32[1024,4096]{1,0:T(8,128)} %get-tuple-element.8, f32[1024]{0:T(1024)S(1)} %pmax.7), kind=kLoop, calls=%fused_computation.3 | loop fusion | flops 8387584 | bytes 16785408 | tf_op jit(solution)/shard_map/reduce_sum | solution.py:25
  207.4 62.7 %psum.14 = f32[1024]{0:T(1024)S(1)} all-reduce(f32[1024]{0:T(1024)S(1)} %add.34), channel_id=1, replica_groups=mesh['dp'=8,'queue'=16] {'dp','queue'}, use_global_device_ids=true, to_apply=%region_6.0 | all-reduce | flops 1024 | bytes 8192 | tf_op jit(solution)/shard_map/psum | solution.py:26
  270.2 0.0 all-gather.5.cloned.1.call-done
  270.2 2.2 gather_fusion
  272.4 0.9 fusion.7
  273.3 0.7 subtract_reduce_fusion
  273.9 64.7 %psum.15 = f32[]{:T(128)} all-reduce(f32[]{:T(128)} %get-tuple-element.3), channel_id=1, replica_groups=mesh['dp'=8,'queue'=16] {'dp','queue'}, use_global_device_ids=true, to_apply=%region_9.10 | all-reduce | flops 1 | bytes 8 | tf_op jit(solution)/shard_map/psum | solution.py:51
  339.3 12.4 %scatter_fusion = bf16[4096,768]{1,0:T(8,128)(2,1)} fusion(bf16[4096,768]{1,0:T(8,128)(2,1)} %copy.11, s32[1024]{0:T(1024)S(1)} %compare_select_fusion, bf16[1024,768]{1,0:T(8,128)(2,1)} %all-gather.5.cloned.1.call-done), kind=kCustom, calls=%fused_computation.1 | custom fusion | bytes 4722688 | tf_op jit(solution)/shard_map/scatter | solution.py:57
  351.8 0.0 reduce-scatter.2.cloned.1.call-done
  351.8 1.4 convert_subtract_fusion
  (6 shorter events, 0.1 us)
Async XLA Ops:
  7.2 34.1 %all-gather.3.cloned.1.call-start = ((), (), s32[]{:S(2)}) async-start(), calls=%async_computation.1 | async-start | bytes 1769472 | tf_op jit(solution)/shard_map/all_gather | solution.py:14
  13.1 257.0 %all-gather.5.cloned.1.call-start = ((), (), s32[]{:S(2)}) async-start(), calls=%async_computation.3 | async-start | bytes 1585152 | tf_op jit(solution)/shard_map/all_gather | solution.py:16
  13.9 40.7 %copy-start.1 = (bf16[8,768]{1,0:T(8,128)(2,1)S(1)}, bf16[8,768]{1,0:T(8,128)(2,1)}, u32[]{:S(2)}) copy-start(bf16[8,768]{1,0:T(8,128)(2,1)} %param.6) | copy-start | bytes 36868
  13.9 337.9 %reduce-scatter.2.cloned.1.call-start = ((), (), s32[]{:S(2)}) async-start(), calls=%async_computation.2 | async-start | bytes 3170304 | tf_op jit(solution)/shard_map/reduce_scatter | solution.py:32
  41.3 13.3 %copy-start = (bf16[1024,768]{1,0:T(8,128)(2,1)S(1)}, bf16[1024,768]{1,0:T(8,128)(2,1)}, u32[]{:S(2)}) copy-start(bf16[1024,768]{1,0:T(8,128)(2,1)} %all-gather.3.cloned.1.call-done) | copy-start | bytes 4718596
  132.3 2.4 copy-start.3
  132.4 66.7 %copy-start.2 = (s32[128]{0:T(128)S(1)}, s32[128]{0:T(128)}, u32[]{:S(2)}) copy-start(s32[128]{0:T(128)} %param.9) | copy-start | bytes 1540
Sparse Core Ops, SparseCore 0:
  13.2 27.9 all-gather.2
  44.0 64.3 all-gather.4
  134.8 205.3 reduce-scatter.1
where the time goes:
time: 362 us; the launch traced here: 361 us
  blocking collectives  256 us (71%)
  matrix products  28.4 us (8%)
  waiting for transfers between devices  28 us (8%)
  local copies, waits for them, and re-layouts  20.8 us (6%)
  between operations  15.6 us (4%)
  other arithmetic  11.4 us (3%)
    pmax x1, blocking collectives, shards(): row_top = lax.pmax(local_top, ('dp', 'queue'))  64.9 us
    psum x1, blocking collectives, shards(): loss_sum = lax.psum(loss_part, ('dp', 'queue'))  64.7 us
    unnamed x1, blocking collectives  64.1 us
    psum x1, blocking collectives, shards(): sum_exp = lax.psum(local_sum, ('dp', 'queue'))  62.7 us
    all_gather x1, waiting for transfers between devices, shards(): all_queries = lax.all_gather(queries, 'dp', axis=0, tiled=True)  27.3 us
    dot_general x2, matrix products, score_rows(): lax.dot_general(query_rows, key_rows, (((1,), (1,)), ((), ())), preferred...  13.8 us
    scatter x1, local copies, waits for them, and re-layouts, shards(): new_queue = queue_keys.at[target].set(fresh_all, mode='drop')  12.4 us
    dot_general x1, matrix products, shards(): jnp.dot(queue_weights, queue_keys, preferred_element_type=jnp.float32)  12.3 us
  transfers between devices with their start and end apart: 3, of which 1 were waited for; matrix products, arithmetic and copies ran while one was open for 15% of the time, Pallas kernels for 0%

commit v1 on v0

--- a/solution.py
+++ b/solution.py
@@ -23,7 +23,7 @@
     queue_exp = jnp.exp(queue_scores - row_top[:, None])
     fresh_exp = jnp.exp(fresh_scores - row_top[:, None])
     local_sum = jnp.sum(queue_exp, axis=1) + jnp.sum(fresh_exp, axis=1)
-    sum_exp = lax.psum(local_sum, ("dp", "queue"))
+    sum_exp = lax.psum(lax.psum(local_sum, "queue"), "dp")
     queue_weights = queue_exp.astype(jnp.bfloat16)
     fresh_weights = fresh_exp.astype(jnp.bfloat16)
     dp_size = lax.axis_size("dp")

time: 362 us -> 351 us (0.970)
  blocking collectives: 256 us -> 242 us
    psum x1 -> x2, blocking collectives: 62.7 us -> 50.5 us  [shards(): sum_exp = lax.psum(lax.psum(local_sum, 'queue'), 'dp')]
  transfers between devices with their start and end apart: 3 -> 3, of which waited for: 1 -> 2; matrix products, arithmetic and copies ran while one was open for 15% -> 15% of each run, Pallas kernels for 0% -> 0%
where the time goes in v1:
time: 351 us; the launch traced here: 349 us
  blocking collectives  242 us (69%)
  waiting for transfers between devices  30.4 us (9%)
  matrix products  28.4 us (8%)
  local copies, waits for them, and re-layouts  20.8 us (6%)
  between operations  15.6 us (4%)
  other arithmetic  11.4 us (3%)
    pmax x1, blocking collectives, shards(): row_top = lax.pmax(local_top, ('dp', 'queue'))  64.9 us
    unnamed x1, blocking collectives  64.1 us
    psum x1, blocking collectives, shards(): loss_sum = lax.psum(loss_part, ('dp', 'queue'))  62.6 us
    psum x2, blocking collectives, shards(): sum_exp = lax.psum(lax.psum(local_sum, 'queue'), 'dp')  50.5 us
    all_gather x1, waiting for transfers between devices, shards(): all_queries = lax.all_gather(queries, 'dp', axis=0, tiled=True)  27.3 us
    dot_general x2, matrix products, score_rows(): lax.dot_general(query_rows, key_rows, (((1,), (1,)), ((), ())), preferred...  13.8 us
    scatter x1, local copies, waits for them, and re-layouts, shards(): new_queue = queue_keys.at[target].set(fresh_all, mode='drop')  12.4 us
    dot_general x1, matrix products, shards(): jnp.dot(queue_weights, queue_keys, preferred_element_type=jnp.float32)  12.3 us
  transfers between devices with their start and end apart: 3, of which 2 were waited for; matrix products, arithmetic and copies ran while one was open for 15% of the time, Pallas kernels for 0%

profile of v1, /device:TPU:1, one launch (start us, length us, event | category | flops | bytes accessed | tf_op | source)
XLA Modules:
  0.0 348.9 jit_solution(5618170271558579692)
XLA Ops:
  7.2 0.0 all-gather.3.cloned.1.call-start
  7.2 5.9 %copy.11 = bf16[4096,768]{1,0:T(8,128)(2,1)} copy(bf16[4096,768]{1,0:T(8,128)(2,1)} %param.5) | data formatting | bytes 12582912
  13.1 0.0 all-gather.3.cloned.1.call-update
  13.1 0.0 all-gather.5.cloned.1.call-start
  13.2 0.7 all-gather.5.cloned.1.call-update
  13.9 0.0 copy-start.1
  13.9 0.0 reduce-scatter.2.cloned.1.call-start
  13.9 27.3 %all-gather.3.cloned.1.call-done = bf16[1024,768]{1,0:T(8,128)(2,1)} async-done(((bf16[128,768]{1,0:T(8,128)(2,1)}), bf16[1024,768]{1,0:T(8,128)(2,1)}) %all-gather.3.cloned.1.call-update) | async-done | bytes 1572880 | tf_op jit(solution)/shard_map/all_gather | solution.py:14
  41.3 0.0 copy-start
  41.3 13.3 %fusion.10 = (f32[1024]{0:T(1024)S(1)}, f32[1024,4096]{1,0:T(8,128)}) fusion(bf16[1024,768]{1,0:T(8,128)(2,1)} %all-gather.3.cloned.1.call-done, bf16[4096,768]{1,0:T(8,128)(2,1)} %copy.11), kind=kOutput, calls=%fused_computation.21 | convolution fusion | flops 6446644224 | bytes 24645632 | tf_op jit(solution)/shard_map/dot_general | solution.py:8
  54.6 0.0 copy-done.1
  54.6 0.0 copy-done
  54.6 0.5 fusion.11
  55.1 64.9 %pmax.7 = f32[1024]{0:T(1024)S(1)} all-reduce(f32[1024]{0:T(1024)S(1)} %max.5), channel_id=1, replica_groups=mesh['dp'=8,'queue'=16] {'dp','queue'}, use_global_device_ids=true, to_apply=%region_2.0 | all-reduce | flops 1024 | bytes 8192 | tf_op jit(solution)/shard_map/pmax | solution.py:22
  120.1 12.3 %fusion.2 = f32[1024,768]{1,0:T(8,128)S(1)} fusion(bf16[4096,768]{1,0:T(8,128)(2,1)} %copy.11, f32[1024,4096]{1,0:T(8,128)} %get-tuple-element.8, f32[1024]{0:T(1024)S(1)} %pmax.7), kind=kOutput, calls=%fused_computation.5 | convolution fusion | flops 6450839552 | bytes 26218496 | tf_op jit(solution)/shard_map/dot_general | solution.py:33
  132.3 0.0 copy-start.3
  132.4 0.0 copy-start.2
  132.4 2.3 convolution_add_fusion
  134.7 0.0 reduce-scatter.2.cloned.1.call-update
  134.7 0.0 copy-done.3
  134.7 0.2 dynamic-update-slice
  135.0 64.1 %all-reduce = s32[1024]{0:T(1024)S(1)} all-reduce(s32[1024]{0:T(1024)S(1)} %dynamic-update-slice), channel_id=1, replica_groups=mesh['dp'=8,'queue'=16] {'dp','queue'}, use_global_device_ids=true, to_apply=%add | all-reduce | flops 1024 | bytes 8192
  199.1 0.0 copy-done.2
  199.1 0.1 compare_and_fusion
  199.2 8.2 %fusion = f32[1024]{0:T(1024)S(1)} fusion(f32[1024,4096]{1,0:T(8,128)} %get-tuple-element.8, f32[1024]{0:T(1024)S(1)} %pmax.7), kind=kLoop, calls=%fused_computation.3 | loop fusion | flops 8387584 | bytes 16785408 | tf_op jit(solution)/shard_map/reduce_sum | solution.py:25
  207.4 31.1 %psum.21 = f32[1024]{0:T(1024)S(1)} all-reduce(f32[1024]{0:T(1024)S(1)} %add.36), channel_id=1, replica_groups=mesh['dp'=8,'queue'=16] {'queue'}, use_global_device_ids=true, to_apply=%region_6.0 | all-reduce | flops 1024 | bytes 8192 | tf_op jit(solution)/shard_map/psum | solution.py:26
  238.5 19.4 %psum.22 = f32[1024]{0:T(1024)S(1)} all-reduce(f32[1024]{0:T(1024)S(1)} %psum.21), channel_id=1, replica_groups=mesh['dp'=8,'queue'=16] {'dp'}, use_global_device_ids=true, to_apply=%region_7.0 | all-reduce | flops 1024 | bytes 8192 | tf_op jit(solution)/shard_map/psum | solution.py:26
  258.0 0.0 all-gather.5.cloned.1.call-done
  258.0 2.2 gather_fusion
  260.2 0.9 fusion.7
  261.1 0.7 subtract_reduce_fusion
  261.8 62.6 %psum.23 = f32[]{:T(128)} all-reduce(f32[]{:T(128)} %get-tuple-element.3), channel_id=1, replica_groups=mesh['dp'=8,'queue'=16] {'dp','queue'}, use_global_device_ids=true, to_apply=%region_10.11 | all-reduce | flops 1 | bytes 8 | tf_op jit(solution)/shard_map/psum | solution.py:51
  325.0 12.4 %scatter_fusion = bf16[4096,768]{1,0:T(8,128)(2,1)} fusion(bf16[4096,768]{1,0:T(8,128)(2,1)} %copy.11, s32[1024]{0:T(1024)S(1)} %compare_select_fusion, bf16[1024,768]{1,0:T(8,128)(2,1)} %all-gather.5.cloned.1.call-done), kind=kCustom, calls=%fused_computation.1 | custom fusion | bytes 4722688 | tf_op jit(solution)/shard_map/scatter | solution.py:57
  337.5 2.4 reduce-scatter.2.cloned.1.call-done
  339.8 1.4 convert_subtract_fusion
  (6 shorter events, 0.1 us)
Async XLA Ops:
  7.2 34.1 %all-gather.3.cloned.1.call-start = ((), (), s32[]{:S(2)}) async-start(), calls=%async_computation.1 | async-start | bytes 1769472 | tf_op jit(solution)/shard_map/all_gather | solution.py:14
  13.1 244.8 %all-gather.5.cloned.1.call-start = ((), (), s32[]{:S(2)}) async-start(), calls=%async_computation.3 | async-start | bytes 1585152 | tf_op jit(solution)/shard_map/all_gather | solution.py:16
  13.9 40.7 %copy-start.1 = (bf16[8,768]{1,0:T(8,128)(2,1)S(1)}, bf16[8,768]{1,0:T(8,128)(2,1)}, u32[]{:S(2)}) copy-start(bf16[8,768]{1,0:T(8,128)(2,1)} %param.6) | copy-start | bytes 36868
  13.9 325.9 %reduce-scatter.2.cloned.1.call-start = ((), (), s32[]{:S(2)}) async-start(), calls=%async_computation.2 | async-start | bytes 3170304 | tf_op jit(solution)/shard_map/reduce_scatter | solution.py:32
  41.3 13.3 %copy-start = (bf16[1024,768]{1,0:T(8,128)(2,1)S(1)}, bf16[1024,768]{1,0:T(8,128)(2,1)}, u32[]{:S(2)}) copy-start(bf16[1024,768]{1,0:T(8,128)(2,1)} %all-gather.3.cloned.1.call-done) | copy-start | bytes 4718596
  132.3 2.4 copy-start.3
  132.4 66.7 %copy-start.2 = (s32[128]{0:T(128)S(1)}, s32[128]{0:T(128)}, u32[]{:S(2)}) copy-start(s32[128]{0:T(128)} %param.9) | copy-start | bytes 1540
Sparse Core Ops, SparseCore 0:
  13.2 27.9 all-gather.2
  44.0 64.3 all-gather.4
  134.8 204.9 reduce-scatter.1

commit v2 on v0

--- a/solution.py
+++ b/solution.py
@@ -23,7 +23,7 @@
     queue_exp = jnp.exp(queue_scores - row_top[:, None])
     fresh_exp = jnp.exp(fresh_scores - row_top[:, None])
     local_sum = jnp.sum(queue_exp, axis=1) + jnp.sum(fresh_exp, axis=1)
-    sum_exp = lax.psum(local_sum, ("dp", "queue"))
+    sum_exp = jnp.sum(lax.all_gather(local_sum, ("dp", "queue")), axis=0)
     queue_weights = queue_exp.astype(jnp.bfloat16)
     fresh_weights = fresh_exp.astype(jnp.bfloat16)
     dp_size = lax.axis_size("dp")

time: 362 us -> 351 us (0.970)
  blocking collectives: 256 us -> 244 us
    psum x1 -> x0, blocking collectives: 62.7 us -> none  [shards(): sum_exp = lax.psum(local_sum, ('dp', 'queue'))]
    all_gather x0 -> x1, blocking collectives: none -> 50.6 us  [shards(): sum_exp = jnp.sum(lax.all_gather(local_sum, ('dp', 'queue')), axis=0)]
  transfers between devices with their start and end apart: 3 -> 3, of which waited for: 1 -> 2; matrix products, arithmetic and copies ran while one was open for 15% -> 15% of each run, Pallas kernels for 0% -> 0%
where the time goes in v2:
time: 351 us; the launch traced here: 349 us
  blocking collectives  244 us (70%)
  matrix products  28.4 us (8%)
  waiting for transfers between devices  28.2 us (8%)
  local copies, waits for them, and re-layouts  20.9 us (6%)
  between operations  15.7 us (4%)
  other arithmetic  11.4 us (3%)
    pmax x1, blocking collectives, shards(): row_top = lax.pmax(local_top, ('dp', 'queue'))  64.9 us
    psum x1, blocking collectives, shards(): loss_sum = lax.psum(loss_part, ('dp', 'queue'))  64.7 us
    unnamed x1, blocking collectives  64.1 us
    all_gather x1, blocking collectives, shards(): sum_exp = jnp.sum(lax.all_gather(local_sum, ('dp', 'queue')), axis=0)  50.6 us
    all_gather x1, waiting for transfers between devices, shards(): all_queries = lax.all_gather(queries, 'dp', axis=0, tiled=True)  27.3 us
    dot_general x2, matrix products, score_rows(): lax.dot_general(query_rows, key_rows, (((1,), (1,)), ((), ())), preferred...  13.8 us
    scatter x1, local copies, waits for them, and re-layouts, shards(): new_queue = queue_keys.at[target].set(fresh_all, mode='drop')  12.4 us
    dot_general x1, matrix products, shards(): jnp.dot(queue_weights, queue_keys, preferred_element_type=jnp.float32)  12.3 us
  transfers between devices with their start and end apart: 3, of which 2 were waited for; matrix products, arithmetic and copies ran while one was open for 15% of the time, Pallas kernels for 0%

profile of v2, /device:TPU:1, one launch (start us, length us, event | category | flops | bytes accessed | tf_op | source)
XLA Modules:
  0.0 348.9 jit_solution(4218929645868963226)
XLA Ops:
  7.2 0.0 all-gather.4.cloned.1.call-start
  7.2 5.9 %copy.11 = bf16[4096,768]{1,0:T(8,128)(2,1)} copy(bf16[4096,768]{1,0:T(8,128)(2,1)} %param.5) | data formatting | bytes 12582912
  13.1 0.0 all-gather.4.cloned.1.call-update
  13.1 0.0 all-gather.6.cloned.1.call-start
  13.2 0.7 all-gather.6.cloned.1.call-update
  13.9 0.0 copy-start.1
  13.9 0.0 reduce-scatter.2.cloned.1.call-start
  13.9 27.3 %all-gather.4.cloned.1.call-done = bf16[1024,768]{1,0:T(8,128)(2,1)} async-done(((bf16[128,768]{1,0:T(8,128)(2,1)}), bf16[1024,768]{1,0:T(8,128)(2,1)}) %all-gather.4.cloned.1.call-update) | async-done | bytes 1572880 | tf_op jit(solution)/shard_map/all_gather | solution.py:14
  41.3 0.0 copy-start
  41.3 13.3 %fusion.10 = (f32[1024]{0:T(1024)S(1)}, f32[1024,4096]{1,0:T(8,128)}) fusion(bf16[1024,768]{1,0:T(8,128)(2,1)} %all-gather.4.cloned.1.call-done, bf16[4096,768]{1,0:T(8,128)(2,1)} %copy.11), kind=kOutput, calls=%fused_computation.21 | convolution fusion | flops 6446644224 | bytes 24645632 | tf_op jit(solution)/shard_map/dot_general | solution.py:8
  54.6 0.0 copy-done.1
  54.6 0.0 copy-done
  54.6 0.5 fusion.11
  55.1 64.9 %pmax.7 = f32[1024]{0:T(1024)S(1)} all-reduce(f32[1024]{0:T(1024)S(1)} %max.5), channel_id=1, replica_groups=mesh['dp'=8,'queue'=16] {'dp','queue'}, use_global_device_ids=true, to_apply=%region_2.0 | all-reduce | flops 1024 | bytes 8192 | tf_op jit(solution)/shard_map/pmax | solution.py:22
  120.1 12.3 %fusion.2 = f32[1024,768]{1,0:T(8,128)S(1)} fusion(bf16[4096,768]{1,0:T(8,128)(2,1)} %copy.11, f32[1024,4096]{1,0:T(8,128)} %get-tuple-element.8, f32[1024]{0:T(1024)S(1)} %pmax.7), kind=kOutput, calls=%fused_computation.5 | convolution fusion | flops 6450839552 | bytes 26218496 | tf_op jit(solution)/shard_map/dot_general | solution.py:33
  132.3 0.0 copy-start.3
  132.4 0.0 copy-start.2
  132.4 2.3 convolution_add_fusion
  134.7 0.0 reduce-scatter.2.cloned.1.call-update
  134.7 0.0 copy-done.3
  134.7 0.2 dynamic-update-slice
  135.0 64.1 %all-reduce = s32[1024]{0:T(1024)S(1)} all-reduce(s32[1024]{0:T(1024)S(1)} %dynamic-update-slice), channel_id=1, replica_groups=mesh['dp'=8,'queue'=16] {'dp','queue'}, use_global_device_ids=true, to_apply=%add | all-reduce | flops 1024 | bytes 8192
  199.1 0.0 copy-done.2
  199.1 0.1 compare_and_fusion
  199.2 8.2 %fusion = f32[1024]{0:T(1024)S(1)} fusion(f32[1024,4096]{1,0:T(8,128)} %get-tuple-element.8, f32[1024]{0:T(1024)S(1)} %pmax.7), kind=kLoop, calls=%fused_computation.3 | loop fusion | flops 8387584 | bytes 16785408 | tf_op jit(solution)/shard_map/reduce_sum | solution.py:25
  207.4 50.6 %all-gather = f32[131072]{0:T(1024)S(1)} all-gather(f32[1024]{0:T(1024)S(1)} %add.42), channel_id=2, replica_groups=mesh['dp'=8,'queue'=16] {'dp','queue'}, dimensions={0}, use_global_device_ids=true | all-gather | bytes 528384 | tf_op jit(solution)/shard_map/all_gather | solution.py:26
  258.0 0.1 reshape.41
  258.2 0.0 all-gather.6.cloned.1.call-done
  258.2 2.2 gather_fusion
  260.4 0.9 fusion.7
  261.3 0.7 subtract_reduce_fusion
  262.0 64.7 %psum.7 = f32[]{:T(128)} all-reduce(f32[]{:T(128)} %get-tuple-element.3), channel_id=1, replica_groups=mesh['dp'=8,'queue'=16] {'dp','queue'}, use_global_device_ids=true, to_apply=%region_9.10 | all-reduce | flops 1 | bytes 8 | tf_op jit(solution)/shard_map/psum | solution.py:51
  327.3 12.4 %scatter_fusion = bf16[4096,768]{1,0:T(8,128)(2,1)} fusion(bf16[4096,768]{1,0:T(8,128)(2,1)} %copy.11, s32[1024]{0:T(1024)S(1)} %compare_select_fusion, bf16[1024,768]{1,0:T(8,128)(2,1)} %all-gather.6.cloned.1.call-done), kind=kCustom, calls=%fused_computation.1 | custom fusion | bytes 4722688 | tf_op jit(solution)/shard_map/scatter | solution.py:57
  339.7 0.1 reduce-scatter.2.cloned.1.call-done
  339.8 1.4 convert_subtract_fusion
  (7 shorter events, 0.1 us)
Async XLA Ops:
  7.2 34.1 %all-gather.4.cloned.1.call-start = ((), (), s32[]{:S(2)}) async-start(), calls=%async_computation.1 | async-start | bytes 1769472 | tf_op jit(solution)/shard_map/all_gather | solution.py:14
  13.1 245.0 %all-gather.6.cloned.1.call-start = ((), (), s32[]{:S(2)}) async-start(), calls=%async_computation.3 | async-start | bytes 1585152 | tf_op jit(solution)/shard_map/all_gather | solution.py:16
  13.9 40.7 %copy-start.1 = (bf16[8,768]{1,0:T(8,128)(2,1)S(1)}, bf16[8,768]{1,0:T(8,128)(2,1)}, u32[]{:S(2)}) copy-start(bf16[8,768]{1,0:T(8,128)(2,1)} %param.6) | copy-start | bytes 36868
  13.9 325.9 %reduce-scatter.2.cloned.1.call-start = ((), (), s32[]{:S(2)}) async-start(), calls=%async_computation.2 | async-start | bytes 3170304 | tf_op jit(solution)/shard_map/reduce_scatter | solution.py:32
  41.3 13.3 %copy-start = (bf16[1024,768]{1,0:T(8,128)(2,1)S(1)}, bf16[1024,768]{1,0:T(8,128)(2,1)}, u32[]{:S(2)}) copy-start(bf16[1024,768]{1,0:T(8,128)(2,1)} %all-gather.4.cloned.1.call-done) | copy-start | bytes 4718596
  132.3 2.4 copy-start.3
  132.4 66.7 %copy-start.2 = (s32[128]{0:T(128)S(1)}, s32[128]{0:T(128)}, u32[]{:S(2)}) copy-start(s32[128]{0:T(128)} %param.9) | copy-start | bytes 1540
Sparse Core Ops, SparseCore 0:
  13.2 27.9 all-gather.3
  44.0 64.3 all-gather.5
  134.8 204.9 reduce-scatter.1
